TPU v7x, 32 devices: a whole 2x2x4 slice. The times are simulated.
32 devices in a mesh: rep: 2 (over y), hid: 8 (over z, x), wid: 2 (over core).
Axes of the slice: x: 2, y: 2, z: 4, core: 2. Of those that a mesh axis runs over, the one named last changes fastest.
Arguments:
- states: float32 [32, 8192], P(('rep', 'hid'), 'wid'), parts along dimension 0, may hold values from -6 to 6
- norm_gain: float32 [8192], P('wid'), may hold values from 0.25 to 1.75
- gate_weight: bfloat16 [8192, 16384], P('wid', 'hid'), may hold values from -0.0625 to 0.0625
- up_weight: bfloat16 [8192, 16384], P('wid', 'hid'), may hold values from -0.0625 to 0.0625
- down_weight: bfloat16 [16384, 8192], P('hid', 'wid'), may hold values from -0.046875 to 0.046875
Outputs:
- updated: float32 [32, 8192], P(('rep', 'hid'), 'wid'), parts along dimension 0
There are 2 independent parts, one for each index of `rep`. A program takes and returns all parts, laid end to end along the dimension named above; an argument that names none is the same for every part. Nothing has to cross between parts.
All inputs are finite; a program needn't handle non-finite values.
Results may differ from a plain program's by a relative error of at most 0.0029.
Values may be sent and summed in bfloat16 or wider, within the bound.
A program may use at most 128 MiB of HBM per device.

v0:
```python
import jax
import jax.numpy as jnp
from jax import lax
from jax.sharding import PartitionSpec as P

D = 8192


def both_parts(block, gate_weight, up_weight):
    gate_part = jnp.dot(block, gate_weight, preferred_element_type=jnp.float32)
    up_part = jnp.dot(block, up_weight, preferred_element_type=jnp.float32)
    return jnp.concatenate([gate_part, up_part], axis=1)


def activate(summed, width):
    return (jax.nn.silu(summed[:, :width]) * summed[:, width:]).astype(jnp.bfloat16)


def local(states, norm_gain, gate_weight, up_weight, down_weight):
    local_power = jnp.sum(states * states, axis=1)
    power = lax.psum(local_power, "wid") / D
    normed = (states * norm_gain[None, :] * lax.rsqrt(power + 1e-05)[:, None]).astype(jnp.bfloat16)
    width = gate_weight.shape[1]
    partial_value = both_parts(
        lax.all_gather(normed, "hid", axis=0, tiled=True), gate_weight, up_weight
    )
    summed = lax.psum(partial_value, "wid")
    hidden = activate(summed, width)
    mixed = lax.psum_scatter(
        jnp.dot(hidden, down_weight, preferred_element_type=jnp.float32),
        "hid",
        scatter_dimension=0,
        tiled=True,
    )
    return states + mixed


def solution(mesh):
    return jax.shard_map(
        local,
        mesh=mesh,
        in_specs=(
            P(("rep", "hid"), "wid"),
            P("wid"),
            P("wid", "hid"),
            P("wid", "hid"),
            P("hid", "wid"),
        ),
        out_specs=P(("rep", "hid"), "wid"),
        check_vma=False,
    )
```

profile of v0, /device:TPU:0, one launch (start us, length us, event | category | flops | bytes accessed | tf_op | source)
XLA Modules:
  0.0 165.8 jit_solution(5688162967370934781)
XLA Ops:
  6.5 0.0 all-reduce.4.cloned.1.call-start
  6.5 0.9 multiply_reduce_fusion
  7.4 2.6 %psum.14 = f32[2]{0:T(128)S(1)} all-reduce(f32[2]{0:T(128)S(1)} %multiply_reduce_fusion), channel_id=1, replica_groups=mesh['rep'=2,'hid'=8,'wid'=2] {'wid'}, use_global_device_ids=true, to_apply=%region_1.0 | all-reduce | flops 2 | bytes 16 | tf_op jit(solution)/shard_map/psum | solution.py:21
  10.1 0.8 fusion.4
  10.9 32.2 %all-gather = bf16[8,2,4096]{2,1,0:T(2,128)(2,1)S(1)} all-gather(bf16[1,2,4096]{2,1,0:T(2,128)(2,1)S(1)} %fusion.4), channel_id=1, replica_groups=mesh['rep'=2,'hid'=8,'wid'=2] {'hid'}, dimensions={0}, use_global_device_ids=true | all-gather | bytes 147456 | tf_op jit(solution)/shard_map/all_gather | solution.py:25
  43.1 0.1 reshape.3
  43.2 0.0 copy-start
  43.2 8.2 %fusion.6 = f32[16,2048]{1,0:T(8,128)S(1)} fusion(bf16[16,4096]{1,0:T(8,128)(2,1)S(1)} %reshape.3, bf16[4096,2048]{1,0:T(8,128)(2,1)} %param.7), kind=kOutput, calls=%fused_computation.11 | convolution fusion | flops 268435456 | bytes 17039360 | tf_op jit(solution)/shard_map/dot_general | solution.py:10
  51.4 2.3 %copy-done = bf16[4096,2048]{1,0:T(8,128)(2,1)S(1)} copy-done((bf16[4096,2048]{1,0:T(8,128)(2,1)S(1)}, bf16[4096,2048]{1,0:T(8,128)(2,1)}, u32[]{:S(2)}) %copy-start) | copy-done | bytes 16777240
  53.7 2.3 %fusion.7 = f32[16,2048]{1,0:T(8,128)S(1)} fusion(bf16[16,4096]{1,0:T(8,128)(2,1)S(1)} %reshape.3, bf16[4096,2048]{1,0:T(8,128)(2,1)S(1)} %copy-done), kind=kOutput, calls=%fused_computation.12 | convolution fusion | flops 268435456 | bytes 17039360 | tf_op jit(solution)/shard_map/dot_general | solution.py:11
  56.0 0.0 copy-start.2
  56.0 0.0 copy-start.1
  56.0 0.7 pad_maximum_fusion
  56.7 0.0 all-reduce.4.cloned.1.call-update
  56.7 0.0 all-reduce.6.cloned.1.call-start
  56.8 19.3 %all-reduce.4.cloned.1.call-done = f32[16,4096]{1,0:T(8,128)} async-done(((f32[16,4096]{1,0:T(8,128)}), f32[16,4096]{1,0:T(8,128)}) %all-reduce.4.cloned.1.call-update) | async-done | bytes 262160 | tf_op jit(solution)/shard_map/psum | solution.py:27
  76.1 8.9 %fusion.1 = f32[16,4096]{1,0:T(8,128)} fusion(bf16[2048,4096]{1,0:T(8,128)(2,1)} %param.9, f32[16,4096]{1,0:T(8,128)} %all-reduce.4.cloned.1.call-done), kind=kOutput, calls=%fused_computation.3 | convolution fusion | flops 268632064 | bytes 17301504 | tf_op jit(solution)/shard_map/dot_general | solution.py:30
  85.0 0.0 all-reduce.6.cloned.1.call-update
  85.0 0.0 copy-done.2
  85.1 0.6 dynamic-slice
  86.3 71.1 %all-reduce.6.cloned.1.call-done = f32[16,4096]{1,0:T(8,128)} async-done(((f32[16,4096]{1,0:T(8,128)}), f32[16,4096]{1,0:T(8,128)}) %all-reduce.6.cloned.1.call-update) | async-done | bytes 262160
  157.4 0.0 copy-done.1
  157.4 1.5 dynamic-slice_add_fusion
  (1 shorter events, 0.0 us)
Async XLA Ops:
  6.5 69.6 %all-reduce.4.cloned.1.call-start = ((), (), s32[]{:S(2)}) async-start(), calls=%async_computation | async-start | bytes 524288 | tf_op jit(solution)/shard_map/psum | solution.py:27
  43.2 10.5 %copy-start = (bf16[4096,2048]{1,0:T(8,128)(2,1)S(1)}, bf16[4096,2048]{1,0:T(8,128)(2,1)}, u32[]{:S(2)}) copy-start(bf16[4096,2048]{1,0:T(8,128)(2,1)} %param.8) | copy-start | bytes 50331652
  56.0 29.1 %copy-start.2 = (u32[32]{0:T(128)S(1)}, u32[32]{0:T(128)}, u32[]{:S(2)}) copy-start(u32[32]{0:T(128)} %constant.13) | copy-start | bytes 388
  56.0 101.4 %copy-start.1 = (f32[2,4096]{1,0:T(2,128)S(1)}, f32[2,4096]{1,0:T(2,128)}, u32[]{:S(2)}) copy-start(f32[2,4096]{1,0:T(2,128)} %param.5) | copy-start | bytes 98308
  56.7 100.7 %all-reduce.6.cloned.1.call-start = ((), (), s32[]{:S(2)}) async-start(), calls=%async_computation.1 | async-start | bytes 524288
Sparse Core Ops, SparseCore 0:
  56.9 19.2 all-reduce.3
  85.2 72.2 all-reduce.5
where the time goes:
time: 166 us
  waiting for transfers between devices  90.5 us (55%)
  blocking collectives  34.8 us (21%)
  matrix products  19.4 us (12%)
  between operations  14.1 us (8%)
  other arithmetic  4.02 us (2%)
  local copies, waits for them, and re-layouts  2.98 us (2%)
    unnamed x3, waiting for transfers between devices  71.2 us
    all_gather x1, blocking collectives, local(): lax.all_gather(normed, 'hid', axis=0, tiled=True)  32.2 us
    psum x1, waiting for transfers between devices, local(): summed = lax.psum(partial_value, 'wid')  19.3 us
    dot_general x1, matrix products, local(): jnp.dot(hidden, down_weight, preferred_element_type=jnp.float32)  8.91 us
    dot_general x1, matrix products, both_parts(): gate_part = jnp.dot(block, gate_weight, preferred_element_type=jnp.float32)  8.2 us
  transfers between devices with their start and end apart: 2, of which 2 were waited for; matrix products, arithmetic and copies ran while one was open for 0% of the time, Pallas kernels for 0%

commit v1 on v0

v1 whole, which is shorter than its diff:
```python
import functools

import jax
import jax.numpy as jnp
from jax import lax
from jax.experimental import pallas as pl
from jax.experimental.pallas import tpu as pltpu
from jax.sharding import PartitionSpec as P

MESH = pl.DeviceIdType.MESH
F32 = jnp.float32
BF16 = jnp.bfloat16
GATHER_CHUNKS = 4
DOWN_CHUNKS = 4
WIDTH = 512


def kernel(
    n, features, states, gain, gate_hbm, up_hbm, down_hbm, out,
    gate_w, up_w, down_w, x_own, x_all, pow_own, pow_all, pow_mine, pow_other,
    part, part_other, hidden, y_part, y_all,
    w_sem, d_sem, x_send, x_recv, p_send, p_recv, q_send, q_recv, e_send, e_recv, y_send, y_recv,
):
    me = lax.axis_index("hid")
    core = lax.axis_index("wid")
    partner = {"wid": 1 - core}
    chunks, depth, _ = gate_w.shape
    cols, _, span = down_w.shape
    blocks, _, streams, width = part.shape
    rows = states.shape[0]

    barrier = pltpu.get_barrier_semaphore()

    def every_peer(body):
        def step(offset, carry):
            body(lax.rem(me + offset, n))
            return carry

        lax.fori_loop(1, n, step, 0, unroll=n <= 8)

    def greet(peer):
        pl.semaphore_signal(barrier, inc=1, device_id={"hid": peer}, device_id_type=MESH)

    every_peer(greet)
    pl.semaphore_signal(barrier, inc=1, device_id=partner, device_id_type=MESH)

    def gate_copy(c):
        return pltpu.make_async_copy(gate_hbm.at[pl.ds(c * depth, depth)], gate_w.at[c], w_sem.at[0, c])

    def up_copy(c):
        return pltpu.make_async_copy(up_hbm.at[pl.ds(c * depth, depth)], up_w.at[c], w_sem.at[1, c])

    def down_copy(j):
        return pltpu.make_async_copy(down_hbm.at[:, pl.ds(j * span, span)], down_w.at[j], d_sem.at[j])

    for c in range(chunks):
        gate_copy(c).start()
        up_copy(c).start()
    for j in range(cols):
        down_copy(j).start()

    power = jnp.zeros((rows, 1), F32)
    for c in range(chunks):
        piece = states[:, c * depth:(c + 1) * depth]
        power = power + jnp.sum(piece * piece, axis=1, keepdims=True)
        scaled = (piece * gain[:, c * depth:(c + 1) * depth]).astype(BF16)
        x_own[c] = scaled
        x_all[c, me] = scaled
    power = jnp.broadcast_to(power, (rows, 128))
    pow_own[...] = power
    pow_all[me] = power

    pl.semaphore_wait(barrier, n)

    def send_x(c):
        def one(peer):
            pltpu.make_async_remote_copy(
                src_ref=x_own.at[c], dst_ref=x_all.at[c, me],
                send_sem=x_send.at[c], recv_sem=x_recv.at[c],
                device_id={"hid": peer}, device_id_type=MESH,
            ).start()

        every_peer(one)

    def send_power(peer):
        pltpu.make_async_remote_copy(
            src_ref=pow_own, dst_ref=pow_all.at[me],
            send_sem=p_send, recv_sem=p_recv,
            device_id={"hid": peer}, device_id_type=MESH,
        ).start()

    for c in range(chunks):
        send_x(c)
    every_peer(send_power)

    def wait_bytes(ref, sem):
        pltpu.make_async_copy(ref, ref, sem).wait()

    def exchange(b):
        return pltpu.make_async_remote_copy(
            src_ref=part.at[b], dst_ref=part_other.at[b],
            send_sem=e_send.at[b], recv_sem=e_recv.at[b],
            device_id=partner, device_id_type=MESH,
        )

    swap_power = pltpu.make_async_remote_copy(
        src_ref=pow_mine, dst_ref=pow_other, send_sem=q_send, recv_sem=q_recv,
        device_id=partner, device_id_type=MESH,
    )

    for c in range(chunks):
        wait_bytes(x_all.at[c, pl.ds(0, n - 1)], x_recv.at[c])
        x = x_all[c].reshape(streams, depth)
        gate_copy(c).wait()
        up_copy(c).wait()
        if c == chunks - 1:
            wait_bytes(pow_all.at[pl.ds(0, n - 1)], p_recv)
            pow_mine[...] = pow_all[...].reshape(streams, 128)
            swap_power.start()
        for b in range(blocks):
            for which, weight in ((0, gate_w), (1, up_w)):
                product = jnp.dot(x, weight[c, :, b * width:(b + 1) * width], preferred_element_type=F32)
                if c == 0:
                    part[b, which] = product
                else:
                    part[b, which] += product
            if c == chunks - 1:
                exchange(b).start()

    swap_power.wait_recv()
    mean = (pow_mine[:, :1] + pow_other[:, :1]) / features
    scale = lax.rsqrt(mean + 1e-5)
    for b in range(blocks):
        exchange(b).wait_recv()
        gate = (part[b, 0] + part_other[b, 0]) * scale
        up = (part[b, 1] + part_other[b, 1]) * scale
        hidden[:, b * width:(b + 1) * width] = (gate / (1.0 + jnp.exp(-gate)) * up).astype(BF16)

    h = hidden[...]
    step = min(span, WIDTH)
    for j in range(cols):
        down_copy(j).wait()
        for s in range(0, span, step):
            y = jnp.dot(h, down_w[j, :, s:s + step], preferred_element_type=F32)
            y_part[j, :, :, s:s + step] = y.reshape(n, rows, step).astype(BF16)
        y_all[j, me] = y_part[j, me]

        def send_y(peer):
            pltpu.make_async_remote_copy(
                src_ref=y_part.at[j, peer], dst_ref=y_all.at[j, me],
                send_sem=y_send.at[j], recv_sem=y_recv.at[j],
                device_id={"hid": peer}, device_id_type=MESH,
            ).start()

        every_peer(send_y)

    for j in range(cols):
        wait_bytes(y_all.at[j, pl.ds(0, n - 1)], y_recv.at[j])
        total = jnp.sum(y_all[j].astype(F32), axis=0)
        out[:, j * span:(j + 1) * span] = states[:, j * span:(j + 1) * span] + total

    for c in range(chunks):
        wait_bytes(x_all.at[c, pl.ds(0, n - 1)], x_send.at[c])
    wait_bytes(pow_all.at[pl.ds(0, n - 1)], p_send)
    swap_power.wait_send()
    for b in range(blocks):
        exchange(b).wait_send()
    for j in range(cols):
        wait_bytes(y_part.at[j, pl.ds(0, n - 1)], y_send.at[j])


def solution(mesh):
    n = mesh.shape["hid"]

    def local(states, norm_gain, gate_weight, up_weight, down_weight):
        rows, half = states.shape
        units = gate_weight.shape[1]
        streams = rows * n
        chunks, cols = GATHER_CHUNKS, DOWN_CHUNKS
        depth, span = half // chunks, half // cols
        width = min(WIDTH, units)
        blocks = units // width
        dma = pltpu.SemaphoreType.DMA
        return pl.pallas_call(
            functools.partial(kernel, n, half * mesh.shape["wid"]),
            out_shape=jax.ShapeDtypeStruct((rows, half), F32),
            in_specs=[pl.BlockSpec(memory_space=pltpu.VMEM)] * 2 + [pl.BlockSpec(memory_space=pl.ANY)] * 3,
            out_specs=pl.BlockSpec(memory_space=pltpu.VMEM),
            scratch_shapes=[
                pltpu.VMEM((chunks, depth, units), BF16),
                pltpu.VMEM((chunks, depth, units), BF16),
                pltpu.VMEM((cols, units, span), BF16),
                pltpu.VMEM((chunks, rows, depth), BF16),
                pltpu.VMEM((chunks, n, rows, depth), BF16),
                pltpu.VMEM((rows, 128), F32),
                pltpu.VMEM((n, rows, 128), F32),
                pltpu.VMEM((streams, 128), F32),
                pltpu.VMEM((streams, 128), F32),
                pltpu.VMEM((blocks, 2, streams, width), F32),
                pltpu.VMEM((blocks, 2, streams, width), F32),
                pltpu.VMEM((streams, units), BF16),
                pltpu.VMEM((cols, n, rows, span), BF16),
                pltpu.VMEM((cols, n, rows, span), BF16),
                dma((2, chunks)),
                dma((cols,)),
                dma((chunks,)),
                dma((chunks,)),
                dma(()),
                dma(()),
                dma(()),
                dma(()),
                dma((blocks,)),
                dma((blocks,)),
                dma((cols,)),
                dma((cols,)),
            ],
            compiler_params=pltpu.CompilerParams(
                collective_id=0, has_side_effects=True, vmem_limit_bytes=67043328
            ),
        )(states, norm_gain.reshape(1, half), gate_weight, up_weight, down_weight)

    return jax.shard_map(
        local,
        mesh=mesh,
        in_specs=(
            P(("rep", "hid"), "wid"),
            P("wid"),
            P("wid", "hid"),
            P("wid", "hid"),
            P("hid", "wid"),
        ),
        out_specs=P(("rep", "hid"), "wid"),
        check_vma=False,
    )
```

time: 166 us -> 30.3 us (0.18)
  waiting for transfers between devices: 90.5 us -> 0 us
  blocking collectives: 34.8 us -> 0 us
  Pallas kernels: 0 us -> 28.7 us
  matrix products: 19.4 us -> 0 us
  between operations: 14.1 us -> 0.01 us
  other arithmetic: 4.02 us -> 0 us
    unnamed x3 -> x0, waiting for transfers between devices: 71.2 us -> none
    all_gather x1 -> x0, blocking collectives: 32.2 us -> none  [local(): lax.all_gather(normed, 'hid', axis=0, tiled=True)]
    pallas_call x0 -> x1, Pallas kernels: none -> 28.7 us  [local(): pl.pallas_call(functools.partial(kernel, n, half * mesh.shape['wid']), ou...]
    dot_general x3 -> x0, matrix products: 19.4 us -> none  [the longest x1 8.91 us: local(): jnp.dot(hidden, down_weight, preferred_element_type=jnp.float32)]
    psum x1 -> x0, waiting for transfers between devices: 19.3 us -> none  [local(): summed = lax.psum(partial_value, 'wid')]
    psum x1 -> x0, blocking collectives: 2.62 us -> none  [local(): power = lax.psum(local_power, 'wid') / D]
  transfers between devices with their start and end apart: 2 -> 0, of which waited for: 2 -> 0; matrix products, arithmetic and copies ran while one was open for 0% -> 0% of each run, Pallas kernels for 0% -> 0%
where the time goes in v1:
time: 30.3 us; the launch traced here: 30 us
  Pallas kernels  28.7 us (95%)
  local copies, waits for them, and re-layouts  1.38 us (5%)
    pallas_call x1, Pallas kernels, local(): pl.pallas_call(functools.partial(kernel, n, half * mesh.shape['wid']), ou...  28.7 us
    unnamed x1, local copies, waits for them, and re-layouts  1.38 us

profile of v1, /device:TPU:0, one launch (start us, length us, event | category | flops | bytes accessed | tf_op | source)
XLA Modules:
  0.0 30.0 jit_solution(15161815252611977213)
XLA Ops:
  0.0 28.7 %shard_map.55 = f32[2,4096]{1,0:T(2,128)} custom-call(f32[2,4096]{1,0:T(2,128)} %states.1, f32[1,4096]{1,0:T(1,128)} %bitcast.1, bf16[4096,2048]{1,0:T(8,128)(2,1)} %gate_hbm.1, bf16[4096,2048]{1,0:T(8,128)(2,1)} %up_hbm.1, bf16[2048,4096]{1,0:T(8,128)(2,1)} %down_hbm.1), custom_call_target="tpu_custom_call" | custom-call | tf_op jit(solution)/shard_map/pallas_call | solution.py:184
  28.7 1.4 %copy.7 = f32[2,4096]{1,0:T(2,128)} copy(f32[2,4096]{1,0:T(2,128)} %shard_map.55) | data formatting | bytes 65536

commit v2 on v1

v2 whole, which is shorter than its diff:
```python
import functools

import jax
import jax.numpy as jnp
from jax import lax
from jax.experimental import pallas as pl
from jax.experimental.pallas import tpu as pltpu
from jax.sharding import PartitionSpec as P

MESH = pl.DeviceIdType.MESH
F32 = jnp.float32
BF16 = jnp.bfloat16
GATHER_CHUNKS = 4
WEIGHT_CHUNKS = 8
DOWN_CHUNKS = 8
AHEAD = 3
FIRST = 3
MIDDLE = 4
WIDTH = 512


def kernel(
    n, features, states_hbm, gain_hbm, gate_hbm, up_hbm, down_hbm, out,
    states, gain, gate_w, up_w, down_w, scaled, x_own, x_all, pow_own, pow_other,
    part, part_other, hidden, y_part, y_all,
    in_sem, w_sem, d_sem, x_send, x_recv, p_send, p_recv, e_send, e_recv, y_send, y_recv,
):
    me = lax.axis_index("hid")
    core = lax.axis_index("wid")
    partner = {"wid": 1 - core}
    steps, depth, _ = gate_w.shape
    chunks, _, piece = x_own.shape
    cols, _, span = down_w.shape
    blocks, _, streams, width = part.shape
    rows = states.shape[0]

    barrier = pltpu.get_barrier_semaphore()

    def every_peer(body):
        def step(offset, carry):
            body(lax.rem(me + offset, n))
            return carry

        lax.fori_loop(1, n, step, 0, unroll=n <= 8)

    def greet(peer):
        pl.semaphore_signal(barrier, inc=1, device_id={"hid": peer}, device_id_type=MESH)

    every_peer(greet)
    pl.semaphore_signal(barrier, inc=1, device_id=partner, device_id_type=MESH)

    load_states = pltpu.make_async_copy(states_hbm, states, in_sem.at[0])
    load_gain = pltpu.make_async_copy(gain_hbm, gain, in_sem.at[1])
    load_states.start()
    load_gain.start()

    def gate_copy(c):
        return pltpu.make_async_copy(gate_hbm.at[pl.ds(c * depth, depth)], gate_w.at[c], w_sem.at[0, c])

    def up_copy(c):
        return pltpu.make_async_copy(up_hbm.at[pl.ds(c * depth, depth)], up_w.at[c], w_sem.at[1, c])

    def down_copy(j):
        return pltpu.make_async_copy(down_hbm.at[:, pl.ds(j * span, span)], down_w.at[j], d_sem.at[j])

    def start_weights(first, last):
        for c in range(first, last):
            gate_copy(c).start()
            up_copy(c).start()

    start_weights(0, FIRST)

    load_states.wait()
    load_gain.wait()
    power = jnp.zeros((rows, 1), F32)
    for c in range(chunks):
        here = slice(c * piece, (c + 1) * piece)
        value = states[:, here]
        power = power + jnp.sum(value * value, axis=1, keepdims=True)
        scaled[:, here] = value * gain[:, here]
    pow_own[...] = jnp.broadcast_to(power, (rows, 128))

    pl.semaphore_wait(barrier, n)

    swap_power = pltpu.make_async_remote_copy(
        src_ref=pow_own, dst_ref=pow_other, send_sem=p_send, recv_sem=p_recv,
        device_id=partner, device_id_type=MESH,
    )
    swap_power.start()

    def wait_bytes(ref, sem):
        pltpu.make_async_copy(ref, ref, sem).wait()

    def exchange(b):
        return pltpu.make_async_remote_copy(
            src_ref=part.at[b], dst_ref=part_other.at[b],
            send_sem=e_send.at[b], recv_sem=e_recv.at[b],
            device_id=partner, device_id_type=MESH,
        )

    start_weights(FIRST, MIDDLE)
    swap_power.wait_recv()
    scale = lax.rsqrt((pow_own[:, :1] + pow_other[:, :1]) / features + 1e-5)
    for c in range(chunks):
        x_own[c] = (scaled[:, c * piece:(c + 1) * piece] * scale).astype(BF16)

        def send_x(peer):
            pltpu.make_async_remote_copy(
                src_ref=x_own.at[c], dst_ref=x_all.at[c, me],
                send_sem=x_send.at[c], recv_sem=x_recv.at[c],
                device_id={"hid": peer}, device_id_type=MESH,
            ).start()

        every_peer(send_x)
        x_all[c, me] = x_own[c]

    start_weights(MIDDLE, steps)
    for j in range(min(AHEAD, cols)):
        down_copy(j).start()

    for c in range(steps):
        whole, inner = divmod(c * depth, piece)
        if inner == 0:
            wait_bytes(x_all.at[whole, pl.ds(0, n - 1)], x_recv.at[whole])
        x = x_all[whole, :, :, inner:inner + depth].reshape(streams, depth)
        gate_copy(c).wait()
        up_copy(c).wait()
        for b in range(blocks):
            for which, weight in ((0, gate_w), (1, up_w)):
                product = jnp.dot(x, weight[c, :, b * width:(b + 1) * width], preferred_element_type=F32)
                if c == 0:
                    part[b, which] = product
                else:
                    part[b, which] += product
            if c == steps - 1:
                exchange(b).start()

    for j in range(cols):
        down_copy(j).wait()
        if j + AHEAD < cols:
            down_copy(j + AHEAD).start()
        if j == 0:
            y = jnp.zeros((streams, span), F32)
            for b in range(blocks):
                exchange(b).wait_recv()
                gate = part[b, 0] + part_other[b, 0]
                up = part[b, 1] + part_other[b, 1]
                h = (gate / (1.0 + jnp.exp(-gate)) * up).astype(BF16)
                hidden[:, b * width:(b + 1) * width] = h
                y = y + jnp.dot(h, down_w[j, b * width:(b + 1) * width, :], preferred_element_type=F32)
        else:
            y = jnp.dot(hidden[...], down_w[j], preferred_element_type=F32)
        y_part[j] = y.reshape(n, rows, span).astype(BF16)

        def send_y(peer):
            pltpu.make_async_remote_copy(
                src_ref=y_part.at[j, peer], dst_ref=y_all.at[j, me],
                send_sem=y_send.at[j], recv_sem=y_recv.at[j],
                device_id={"hid": peer}, device_id_type=MESH,
            ).start()

        every_peer(send_y)
        y_all[j, me] = y_part[j, me]

    for j in range(cols):
        wait_bytes(y_all.at[j, pl.ds(0, n - 1)], y_recv.at[j])
        total = jnp.sum(y_all[j].astype(F32), axis=0)
        out[:, j * span:(j + 1) * span] = states[:, j * span:(j + 1) * span] + total

    for c in range(chunks):
        wait_bytes(x_all.at[c, pl.ds(0, n - 1)], x_send.at[c])
    swap_power.wait_send()
    for b in range(blocks):
        exchange(b).wait_send()
    for j in range(cols):
        wait_bytes(y_part.at[j, pl.ds(0, n - 1)], y_send.at[j])


def solution(mesh):
    n = mesh.shape["hid"]

    def local(states, norm_gain, gate_weight, up_weight, down_weight):
        rows, half = states.shape
        units = gate_weight.shape[1]
        streams = rows * n
        chunks, steps, cols = GATHER_CHUNKS, WEIGHT_CHUNKS, DOWN_CHUNKS
        piece, depth, span = half // chunks, half // steps, half // cols
        width = min(WIDTH, units)
        blocks = units // width
        dma = pltpu.SemaphoreType.DMA
        return pl.pallas_call(
            functools.partial(kernel, n, half * mesh.shape["wid"]),
            out_shape=jax.ShapeDtypeStruct((rows, half), F32),
            in_specs=[pl.BlockSpec(memory_space=pl.ANY)] * 5,
            out_specs=pl.BlockSpec(memory_space=pltpu.VMEM),
            scratch_shapes=[
                pltpu.VMEM((rows, half), F32),
                pltpu.VMEM((1, half), F32),
                pltpu.VMEM((steps, depth, units), BF16),
                pltpu.VMEM((steps, depth, units), BF16),
                pltpu.VMEM((cols, units, span), BF16),
                pltpu.VMEM((rows, half), F32),
                pltpu.VMEM((chunks, rows, piece), BF16),
                pltpu.VMEM((chunks, n, rows, piece), BF16),
                pltpu.VMEM((rows, 128), F32),
                pltpu.VMEM((rows, 128), F32),
                pltpu.VMEM((blocks, 2, streams, width), F32),
                pltpu.VMEM((blocks, 2, streams, width), F32),
                pltpu.VMEM((streams, units), BF16),
                pltpu.VMEM((cols, n, rows, span), BF16),
                pltpu.VMEM((cols, n, rows, span), BF16),
                dma((2,)),
                dma((2, steps)),
                dma((cols,)),
                dma((chunks,)),
                dma((chunks,)),
                dma(()),
                dma(()),
                dma((blocks,)),
                dma((blocks,)),
                dma((cols,)),
                dma((cols,)),
            ],
            compiler_params=pltpu.CompilerParams(
                collective_id=0, has_side_effects=True, vmem_limit_bytes=67043328
            ),
        )(states, norm_gain.reshape(1, half), gate_weight, up_weight, down_weight)

    return jax.shard_map(
        local,
        mesh=mesh,
        in_specs=(
            P(("rep", "hid"), "wid"),
            P("wid"),
            P("wid", "hid"),
            P("wid", "hid"),
            P("hid", "wid"),
        ),
        out_specs=P(("rep", "hid"), "wid"),
        check_vma=False,
    )
```

time: 30.3 us -> 27.9 us (0.921)
  Pallas kernels: 28.7 us -> 26.4 us
    pallas_call x1, Pallas kernels: 28.7 us -> 26.4 us  [local(): pl.pallas_call(functools.partial(kernel, n, half * mesh.shape['wid']), ou...]
where the time goes in v2:
time: 27.9 us; the launch traced here: 27.7 us
  Pallas kernels  26.4 us (95%)
  local copies, waits for them, and re-layouts  1.38 us (5%)
    pallas_call x1, Pallas kernels, local(): pl.pallas_call(functools.partial(kernel, n, half * mesh.shape['wid']), ou...  26.4 us
    unnamed x1, local copies, waits for them, and re-layouts  1.38 us

profile of v2, /device:TPU:0, one launch (start us, length us, event | category | flops | bytes accessed | tf_op | source)
XLA Modules:
  0.0 27.7 jit_solution(6465855369422053470)
XLA Ops:
  0.0 26.4 %shard_map.55 = f32[2,4096]{1,0:T(2,128)} custom-call(f32[2,4096]{1,0:T(2,128)} %states_hbm.1, f32[1,4096]{1,0:T(1,128)} %bitcast.1, bf16[4096,2048]{1,0:T(8,128)(2,1)} %gate_hbm.1, bf16[4096,2048]{1,0:T(8,128)(2,1)} %up_hbm.1, bf16[2048,4096]{1,0:T(8,128)(2,1)} %down_hbm.1), custom_call_target="tpu_custom_call" | custom-call | tf_op jit(solution)/shard_map/pallas_call | solution.py:191
  26.4 1.4 %copy.7 = f32[2,4096]{1,0:T(2,128)} copy(f32[2,4096]{1,0:T(2,128)} %shard_map.55) | data formatting | bytes 65536

commit v3 on v2

--- a/solution.py
+++ b/solution.py
@@ -12,8 +12,8 @@
 BF16 = jnp.bfloat16
 GATHER_CHUNKS = 4
 WEIGHT_CHUNKS = 8
-DOWN_CHUNKS = 8
-AHEAD = 3
+DOWN_CHUNKS = 4
+AHEAD = 2
 FIRST = 3
 MIDDLE = 4
 WIDTH = 512

time: 27.9 us -> 27 us (0.968)
  Pallas kernels: 26.4 us -> 25.4 us
    pallas_call x1, Pallas kernels: 26.4 us -> 25.4 us  [local(): pl.pallas_call(functools.partial(kernel, n, half * mesh.shape['wid']), ou...]
where the time goes in v3:
time: 27 us; the launch traced here: 26.8 us
  Pallas kernels  25.4 us (94%)
  local copies, waits for them, and re-layouts  1.38 us (5%)
    pallas_call x1, Pallas kernels, local(): pl.pallas_call(functools.partial(kernel, n, half * mesh.shape['wid']), ou...  25.4 us
    unnamed x1, local copies, waits for them, and re-layouts  1.38 us

profile of v3, /device:TPU:0, one launch (start us, length us, event | category | flops | bytes accessed | tf_op | source)
XLA Modules:
  0.0 26.8 jit_solution(17382862264742835760)
XLA Ops:
  0.0 25.4 %shard_map.55 = f32[2,4096]{1,0:T(2,128)} custom-call(f32[2,4096]{1,0:T(2,128)} %states_hbm.1, f32[1,4096]{1,0:T(1,128)} %bitcast.1, bf16[4096,2048]{1,0:T(8,128)(2,1)} %gate_hbm.1, bf16[4096,2048]{1,0:T(8,128)(2,1)} %up_hbm.1, bf16[2048,4096]{1,0:T(8,128)(2,1)} %down_hbm.1), custom_call_target="tpu_custom_call" | custom-call | tf_op jit(solution)/shard_map/pallas_call | solution.py:191
  25.4 1.4 %copy.7 = f32[2,4096]{1,0:T(2,128)} copy(f32[2,4096]{1,0:T(2,128)} %shard_map.55) | data formatting | bytes 65536
